TPU v7x, 32 devices: a whole 2x2x4 slice. The times are simulated.
32 devices in a mesh: table: 16 (over z, y, x), narrow: 2 (over core).
Axes of the slice: x: 2, y: 2, z: 4, core: 2. Of those that a mesh axis runs over, the one named last changes fastest.
Arguments:
- table_rows: bfloat16 [16384, 256], P('table'), may hold values from -3 to 3
- accum: float32 [16384], P('table'), may hold values from 1 to 100
- factor_down: bfloat16 [2048, 256], P('narrow'), may hold values from -0.125 to 0.125
- factor_up: bfloat16 [2048, 256], P('narrow'), may hold values from -0.375 to 0.375
- cross_bias: float32 [2048], replicated, may hold values from -3 to 3
- out_weight: bfloat16 [2048], replicated, may hold values from -0.125 to 0.125
- target: float32 [4096], P(('table', 'narrow')), may hold values from 0 to 1
- bag_rows: int32 [512, 512], P(('table', 'narrow')), may hold values from -1 to 1023, as said below
- slot_target: int32 [512, 128], P(('table', 'narrow')), may hold values from -1 to 1023, as said below
Outputs:
- logits: float32 [4096], P(('table', 'narrow'))
- down_grad: float32 [2048, 256], P('narrow')
- up_grad: float32 [2048, 256], P('narrow')
- new_rows: bfloat16 [16384, 256], P('table')
- new_accum: float32 [16384], P(('table', 'narrow'))
Inputs may be any that keep to these rules, and one draw needn't show every extreme that they name: `slot_target`: for each source device (its 16 rows): every bag 0 .. 1023 is named by exactly one slot and the other slots hold -1; in every draw each source device has one window all of whose 128 slots are used. `bag_rows`: A used slot holds 1 to 4 rows of the window first and -1 after them; an unused slot holds -1 only; each source device has a slot with 4 lookups.
All inputs are finite; a program needn't handle non-finite values.
Results may differ from a plain program's by a relative error of at most 0.0077.
Values may be sent and summed in bfloat16 or wider, within the bound.
No kernel may reach another device: no remote copies, remote signals or barrier semaphores. Data moves between devices by JAX's collectives and lax.ppermute only.
A program may use at most 64 MiB of HBM per device.

v0:
```python
import math
import jax
import jax.numpy as jnp
from jax import lax
from jax.sharding import PartitionSpec as P

FEAT = 8
HOT = 4
LEARN_RATE = 0.2
LOSS_SCALE = 32.0
ADA_EPS = 1e-06


def transposed_dot(left, right):
    return lax.dot_general(
        left, right, (((0,), (0,)), ((), ())), preferred_element_type=jnp.float32
    )


def rows_dot(left, right):
    return lax.dot_general(
        left, right, (((1,), (1,)), ((), ())), preferred_element_type=jnp.float32
    )


def local(
    table_rows, accum, factor_down, factor_up, cross_bias, out_weight, target, bag_rows, slot_target
):
    tables = lax.axis_size("table")
    narrows = lax.axis_size("narrow")
    row_dev, emb_width = table_rows.shape
    pools_per = slot_target.shape[1]
    samples = target.shape[0]
    bag_count = samples * FEAT
    slot_count = tables * pools_per
    asked = lax.all_to_all(bag_rows, "table", split_axis=0, concat_axis=0, tiled=True)
    lookup_ids = asked.reshape(slot_count, HOT)
    positions = lax.broadcasted_iota(jnp.int32, (1, row_dev), 1)
    counts = jnp.zeros((slot_count, row_dev), jnp.bfloat16)
    for lookup in range(HOT):
        counts = counts + (lookup_ids[:, lookup : lookup + 1] == positions).astype(jnp.bfloat16)
    pool_sums = jnp.dot(counts, table_rows, preferred_element_type=jnp.float32)
    pool_out = pool_sums.astype(jnp.bfloat16).reshape(tables, pools_per, emb_width)
    arrived = lax.all_to_all(pool_out, "table", split_axis=0, concat_axis=0, tiled=True).reshape(
        slot_count, emb_width
    )
    bag_index = lax.broadcasted_iota(jnp.int32, (bag_count, 1), 0)
    placing = (slot_target.reshape(1, slot_count) == bag_index).astype(jnp.bfloat16)
    pooled_feats = (
        jnp.dot(placing, arrived, preferred_element_type=jnp.float32)
        .astype(jnp.bfloat16)
        .reshape(samples, FEAT * emb_width)
    )
    down_full, up_full = (
        lax.all_gather(factor_down, "narrow", axis=0, tiled=True),
        lax.all_gather(factor_up, "narrow", axis=0, tiled=True),
    )
    hidden = jnp.dot(pooled_feats, down_full, preferred_element_type=jnp.float32).astype(
        jnp.bfloat16
    )
    cross_out = rows_dot(hidden, up_full)
    feats_f = pooled_feats.astype(jnp.float32)
    shifted = cross_out + cross_bias
    mixed_out = feats_f * shifted + feats_f
    weight_f = out_weight.astype(jnp.float32)
    logits = jnp.sum(mixed_out * weight_f, axis=1)
    dlogit = LOSS_SCALE * (jax.nn.sigmoid(logits) - target)
    dmixed = dlogit[:, None] * weight_f
    dcross = (dmixed * feats_f).astype(jnp.bfloat16)
    dhidden = jnp.dot(dcross, up_full, preferred_element_type=jnp.float32).astype(jnp.bfloat16)
    back_term = rows_dot(dhidden, down_full)
    dpooled = (dmixed * (shifted + 1.0) + back_term).astype(jnp.bfloat16)
    narrow_sum = lax.psum_scatter(
        jnp.concatenate(
            [transposed_dot(pooled_feats, dhidden), transposed_dot(dcross, hidden)], axis=1
        ).astype(jnp.bfloat16),
        "narrow",
        scatter_dimension=0,
        tiled=True,
    ).astype(jnp.float32)
    grand_total = lax.psum(narrow_sum, "table")
    batch_all = samples * tables * narrows
    grand_total = grand_total * (1.0 / math.sqrt(batch_all))
    rank_size = factor_down.shape[1]
    down_grad = grand_total[:, :rank_size]
    up_grad = grand_total[:, rank_size:]
    bag_grads = dpooled.reshape(bag_count, emb_width)
    slot_grads = (
        transposed_dot(placing, bag_grads)
        .astype(jnp.bfloat16)
        .reshape(tables, pools_per, emb_width)
    )
    returned = lax.all_to_all(slot_grads, "table", split_axis=0, concat_axis=0, tiled=True).reshape(
        slot_count, emb_width
    )
    local_grad = transposed_dot(counts, returned)
    narrow_index = lax.axis_index("narrow")
    share_size = row_dev // narrows
    row_grad = lax.psum(local_grad.astype(jnp.bfloat16), "narrow").astype(jnp.float32)
    accum_all = accum + jnp.mean(row_grad * row_grad, axis=1)
    new_rows = (
        table_rows.astype(jnp.float32)
        - LEARN_RATE * row_grad * lax.rsqrt(accum_all + ADA_EPS)[:, None]
    ).astype(jnp.bfloat16)
    new_accum = lax.dynamic_slice_in_dim(accum_all, narrow_index * share_size, share_size, 0)
    return (logits, down_grad, up_grad, new_rows, new_accum)


def solution(mesh):
    in_specs = (
        P("table", None),
        P("table"),
        P("narrow", None),
        P("narrow", None),
        P(),
        P(),
        P(("table", "narrow")),
        P(("table", "narrow"), None),
        P(("table", "narrow"), None),
    )
    out_specs = (
        P(("table", "narrow")),
        P("narrow", None),
        P("narrow", None),
        P("table", None),
        P(("table", "narrow")),
    )
    return jax.shard_map(local, mesh=mesh, in_specs=in_specs, out_specs=out_specs, check_vma=False)
```

profile of v0, /device:TPU:0, one launch (start us, length us, event | category | flops | bytes accessed | tf_op | source)
XLA Modules:
  0.0 247.3 jit_solution(3443778541291321474)
XLA Ops:
  7.2 0.8 all_to_all.12
  8.0 15.5 %all_to_all.19 = s32[16,1,512]{2,1,0:T(1,128)S(1)} all-to-all(s32[16,1,512]{2,1,0:T(1,128)S(1)} %all_to_all.12), channel_id=1, replica_groups=mesh['table'=16,'narrow'=2] {'table'}, dimensions={0} | all-to-all | bytes 65536 | tf_op jit(solution)/shard_map/all_to_all | solution.py:36
  23.5 1.1 reshape.40
  24.6 2.0 slice_reduce_fusion.3
  26.6 6.1 %fusion.15 = bf16[2048,256]{1,0:T(8,128)(2,1)} fusion(bf16[1024,256]{1,0:T(8,128)(2,1)S(1)} %copy-done.2, s32[2048]{0:T(1024)S(1)} %get-tuple-element.21, s32[2048]{0:T(1024)S(1)} %get-tuple-element.22, s32[2048]{0:T(1024)S(1)} %get-tuple-element.23, s32[2048]{0:T(1024)S(1)} %get-tuple-element.20), kind=kOutput, calls=%fused_computation.18 | convolution fusion | flops 1107820544 | bytes 1605632 | tf_op jit(solution)/shard_map/dot_general | solution.py:42
  32.7 3.8 %all-to-all-start.1 = ((bf16[16,128,256]{2,1,0:T(8,128)(2,1)}), bf16[16,128,256]{2,1,0:T(8,128)(2,1)S(1)}, u32[]{:S(2)}, u32[]{:S(2)}) async-start(bf16[16,128,256]{2,1,0:T(8,128)(2,1)} %bitcast.1), calls=%async_computation.1 | async-start | bytes 2097152 | tf_op jit(solution)/shard_map/all_to_all | solution.py:44
  36.5 0.7 all-gather.3.cloned.1.call-update
  37.3 0.7 all-gather.5.cloned.1.call-update
  38.0 21.7 %all-to-all-done.1 = bf16[16,128,256]{2,1,0:T(8,128)(2,1)S(1)} async-done(((bf16[16,128,256]{2,1,0:T(8,128)(2,1)}), bf16[16,128,256]{2,1,0:T(8,128)(2,1)S(1)}, u32[]{:S(2)}, u32[]{:S(2)}) %all-to-all-start.1) | async-done | bytes 1048608 | tf_op jit(solution)/shard_map/all_to_all | solution.py:44
  59.8 1.5 fusion.23
  61.2 0.2 reshape.43
  61.5 1.5 convolution_convert_fusion.3
  63.1 2.0 fusion.29
  65.1 0.4 convolution_convert_fusion.2
  65.5 0.5 fusion.19
  66.0 0.2 reshape.44
  66.3 3.3 %fusion.18 = bf16[2048,256]{1,0:T(8,128)(2,1)} fusion(bf16[1024,256]{1,0:T(8,128)(2,1)S(1)} %reshape.44, s32[2048]{0:T(1024)S(1)} %bitcast.22), kind=kOutput, calls=%fused_computation.19 | convolution fusion | flops 1076363264 | bytes 1581056 | tf_op jit(solution)/shard_map/dot_general | solution.py:15
  69.6 5.8 %all-to-all-start.2 = ((bf16[16,128,256]{2,1,0:T(8,128)(2,1)}), bf16[16,128,256]{2,1,0:T(8,128)(2,1)S(1)}, u32[]{:S(2)}, u32[]{:S(2)}) async-start(bf16[16,128,256]{2,1,0:T(8,128)(2,1)} %bitcast.3), calls=%async_computation.3 | async-start | bytes 2097152 | tf_op jit(solution)/shard_map/all_to_all | solution.py:93
  75.6 0.5 convolution_convert_fusion
  76.2 23.0 %all-to-all-done.2 = bf16[16,128,256]{2,1,0:T(8,128)(2,1)S(1)} async-done(((bf16[16,128,256]{2,1,0:T(8,128)(2,1)}), bf16[16,128,256]{2,1,0:T(8,128)(2,1)S(1)}, u32[]{:S(2)}, u32[]{:S(2)}) %all-to-all-start.2) | async-done | bytes 1048608 | tf_op jit(solution)/shard_map/all_to_all | solution.py:93
  99.1 5.5 %fusion.20 = bf16[1024,256]{1,0:T(8,128)(2,1)} fusion(bf16[2048,256]{1,0:T(8,128)(2,1)S(1)} %bitcast.20, s32[2048]{0:T(1024)S(1)} %get-tuple-element.21, s32[2048]{0:T(1024)S(1)} %get-tuple-element.22, s32[2048]{0:T(1024)S(1)} %get-tuple-element.23, s32[2048]{0:T(1024)S(1)} %get-tuple-element.20), kind=kOutput, calls=%fused_computation.31 | convolution fusion | flops 1107558400 | bytes 1605632 | tf_op jit(solution)/shard_map/dot_general | solution.py:15
  104.7 0.5 convolution_convert_fusion.1
  105.2 1.5 pad_maximum_fusion
  106.7 17.0 %all-reduce.3.cloned.1.call-done = bf16[1024,256]{1,0:T(8,128)(2,1)} async-done(((bf16[1024,256]{1,0:T(8,128)(2,1)}), bf16[1024,256]{1,0:T(8,128)(2,1)}) %all-reduce.3.cloned.1.call-update) | async-done | bytes 524304 | tf_op jit(solution)/shard_map/psum | solution.py:99
  123.7 1.3 fusion.24
  125.0 0.7 dynamic_slice.3
  125.7 2.1 fusion.26
  127.8 8.9 %reduce-scatter.2.cloned.1.call-done = bf16[1024,512]{0,1:T(8,128)(2,1)} async-done(((bf16[2048,512]{0,1:T(8,128)(2,1)}), bf16[1024,512]{0,1:T(8,128)(2,1)}) %reduce-scatter.2.cloned.1.call-update) | async-done | bytes 1048592 | tf_op jit(solution)/shard_map/reduce_scatter | solution.py:73
  136.7 100.9 %all-reduce.4 = f32[1024,512]{0,1:T(8,128)S(1)} all-reduce(bf16[1024,512]{0,1:T(8,128)(2,1)} %reduce-scatter.2.cloned.1.call-done), channel_id=1, replica_groups=mesh['table'=16,'narrow'=2] {'table'}, use_global_device_ids=true, to_apply=%region_2.0 | all-reduce | flops 524288 | bytes 3145728 | tf_op jit(solution)/shard_map/psum | solution.py:81
  237.9 0.2 fusion.33
  238.2 1.3 copy.19
  239.5 1.3 copy.18
  (31 shorter events, 0.8 us)
Async XLA Ops:
  24.6 2.0 copy-start.2
  32.7 5.3 %copy-start.4 = (bf16[2048]{0:T(1024)(128)(2,1)S(1)}, bf16[2048]{0:T(1024)(128)(2,1)}, u32[]{:S(2)}) copy-start(bf16[2048]{0:T(1024)(128)(2,1)} %param.14) | copy-start | bytes 12292
  32.7 27.1 %copy-start.7 = (s32[16,128]{1,0:T(8,128)S(1)}, s32[16,128]{1,0:T(8,128)}, u32[]{:S(2)}) copy-start(s32[16,128]{1,0:T(8,128)} %param.17) | copy-start | bytes 24580
  32.7 27.1 %all-to-all-start.1 = ((bf16[16,128,256]{2,1,0:T(8,128)(2,1)}), bf16[16,128,256]{2,1,0:T(8,128)(2,1)S(1)}, u32[]{:S(2)}, u32[]{:S(2)}) async-start(bf16[16,128,256]{2,1,0:T(8,128)(2,1)} %bitcast.1), calls=%async_computation.1 | async-start | bytes 2097152 | tf_op jit(solution)/shard_map/all_to_all | solution.py:44
  36.5 25.0 %all-gather.3.cloned.1.call-start = ((), (), s32[]{:S(2)}) async-start(), calls=%async_computation.4 | async-start | bytes 1572864 | tf_op jit(solution)/shard_map/all_gather | solution.py:55
  37.2 25.9 %all-gather.5.cloned.1.call-start = ((), (), s32[]{:S(2)}) async-start(), calls=%async_computation.5 | async-start | bytes 1572864 | tf_op jit(solution)/shard_map/all_gather | solution.py:56
  61.2 1.9 copy-start.3
  61.5 3.6 %copy-start.8 = (f32[128]{0:T(128)S(1)}, f32[128]{0:T(128)}, u32[]{:S(2)}) copy-start(f32[128]{0:T(128)} %param.15) | copy-start | bytes 1540
  63.1 2.4 copy-start
  63.1 2.0 copy-start.1
  65.1 0.9 copy-start.6
  69.6 29.5 %all-to-all-start.2 = ((bf16[16,128,256]{2,1,0:T(8,128)(2,1)}), bf16[16,128,256]{2,1,0:T(8,128)(2,1)S(1)}, u32[]{:S(2)}, u32[]{:S(2)}) async-start(bf16[16,128,256]{2,1,0:T(8,128)(2,1)} %bitcast.3), calls=%async_computation.3 | async-start | bytes 2097152 | tf_op jit(solution)/shard_map/all_to_all | solution.py:93
  75.4 48.3 %all-reduce.3.cloned.1.call-start = ((), (), s32[]{:S(2)}) async-start(), calls=%async_computation.7 | async-start | bytes 1048576 | tf_op jit(solution)/shard_map/psum | solution.py:99
  104.6 32.1 %reduce-scatter.2.cloned.1.call-start = ((), (), s32[]{:S(2)}) async-start(), calls=%async_computation.6 | async-start | bytes 3145728 | tf_op jit(solution)/shard_map/reduce_scatter | solution.py:73
  106.7 18.3 %copy-start.5 = (f32[1024]{0:T(1024)S(1)}, f32[1024]{0:T(1024)}, u32[]{:S(2)}) copy-start(f32[1024]{0:T(1024)} %param.10) | copy-start | bytes 12292
Sparse Core Ops, SparseCore 0:
  38.9 10.2 all-gather.2
  50.7 10.1 all-gather.4
  104.8 18.9 all-reduce.2
  125.9 10.7 reduce-scatter.1
where the time goes:
time: 248 us; the launch traced here: 247 us
  blocking collectives  116 us (47%)
  waiting for transfers between devices  72.1 us (29%)
  matrix products  21.7 us (9%)
  between operations  14 us (6%)
  starting transfers between devices  9.95 us (4%)
  local copies, waits for them, and re-layouts  7.88 us (3%)
  other arithmetic  5.22 us (2%)
    psum x1, blocking collectives, local(): grand_total = lax.psum(narrow_sum, 'table')  101 us
    all_to_all x1, waiting for transfers between devices, local(): lax.all_to_all(slot_grads, 'table', split_axis=0, concat_axis=0, tiled=True)  23 us
    all_to_all x1, waiting for transfers between devices, local(): lax.all_to_all(pool_out, 'table', split_axis=0, concat_axis=0, tiled=True)  21.7 us
    psum x1, waiting for transfers between devices, local(): lax.psum(local_grad.astype(jnp.bfloat16), 'narrow').astype(jnp.float32)  17 us
    all_to_all x1, blocking collectives, local(): lax.all_to_all(bag_rows, 'table', split_axis=0, concat_axis=0, tiled=True)  15.5 us
    dot_general x4, matrix products, transposed_dot(): lax.dot_general(left, right, (((0,), (0,)), ((), ())), preferred_element_...  9.82 us
    reduce_scatter x1, waiting for transfers between devices, local(): lax.psum_scatter(jnp.concatenate([transposed_dot(pooled_feats, dhidden),...  8.95 us
    dot_general x1, matrix products, local(): pool_sums = jnp.dot(counts, table_rows, preferred_element_type=jnp.float32)  6.07 us
  transfers between devices with their start and end apart: 6, of which 4 were waited for; matrix products, arithmetic and copies ran while one was open for 4% of the time, Pallas kernels for 0%

commit v1 on v0

--- a/solution.py
+++ b/solution.py
@@ -96,7 +96,9 @@
     local_grad = transposed_dot(counts, returned)
     narrow_index = lax.axis_index("narrow")
     share_size = row_dev // narrows
-    row_grad = lax.psum(local_grad.astype(jnp.bfloat16), "narrow").astype(jnp.float32)
+    row_grad = jnp.sum(lax.all_gather(local_grad.astype(jnp.bfloat16), "narrow"), axis=0).astype(
+        jnp.float32
+    )
     accum_all = accum + jnp.mean(row_grad * row_grad, axis=1)
     new_rows = (
         table_rows.astype(jnp.float32)

time: 248 us -> 238 us (0.960)
  waiting for transfers between devices: 72.1 us -> 37.2 us
  blocking collectives: 116 us -> 149 us
  starting transfers between devices: 9.95 us -> 3.95 us
    all_to_all x0 -> x1, blocking collectives: none -> 31.3 us  [local(): lax.all_to_all(slot_grads, 'table', split_axis=0, concat_axis=0, tiled=True)]
    all_to_all x1 -> x0, waiting for transfers between devices: 23 us -> none  [local(): lax.all_to_all(slot_grads, 'table', split_axis=0, concat_axis=0, tiled=True)]
    psum x1 -> x0, waiting for transfers between devices: 17 us -> none  [local(): lax.psum(local_grad.astype(jnp.bfloat16), 'narrow').astype(jnp.float32)]
    all_to_all x1 -> x0, starting transfers between devices: 5.82 us -> none  [local(): lax.all_to_all(slot_grads, 'table', split_axis=0, concat_axis=0, tiled=True)]
    all_gather x0 -> x1, waiting for transfers between devices: none -> 4.78 us  [local(): lax.all_gather(local_grad.astype(jnp.bfloat16), 'narrow')]
  transfers between devices with their start and end apart: 6 -> 5, of which waited for: 4 -> 3; matrix products, arithmetic and copies ran while one was open for 4% -> 4% of each run, Pallas kernels for 0% -> 0%
where the time goes in v1:
time: 238 us; the launch traced here: 237 us
  blocking collectives  149 us (63%)
  waiting for transfers between devices  37.2 us (16%)
  matrix products  20.7 us (9%)
  between operations  14 us (6%)
  local copies, waits for them, and re-layouts  7.88 us (3%)
  other arithmetic  4.89 us (2%)
  starting transfers between devices  3.95 us (2%)
    psum x1, blocking collectives, local(): grand_total = lax.psum(narrow_sum, 'table')  102 us
    all_to_all x1, blocking collectives, local(): lax.all_to_all(slot_grads, 'table', split_axis=0, concat_axis=0, tiled=True)  31.3 us
    all_to_all x1, waiting for transfers between devices, local(): lax.all_to_all(pool_out, 'table', split_axis=0, concat_axis=0, tiled=True)  21.7 us
    all_to_all x1, blocking collectives, local(): lax.all_to_all(bag_rows, 'table', split_axis=0, concat_axis=0, tiled=True)  15.5 us
    reduce_scatter x1, waiting for transfers between devices, local(): lax.psum_scatter(jnp.concatenate([transposed_dot(pooled_feats, dhidden),...  9.23 us
    dot_general x4, matrix products, transposed_dot(): lax.dot_general(left, right, (((0,), (0,)), ((), ())), preferred_element_...  8.9 us
    dot_general x1, matrix products, local(): pool_sums = jnp.dot(counts, table_rows, preferred_element_type=jnp.float32)  6.07 us
    all_gather x1, waiting for transfers between devices, local(): lax.all_gather(local_grad.astype(jnp.bfloat16), 'narrow')  4.78 us
  transfers between devices with their start and end apart: 5, of which 3 were waited for; matrix products, arithmetic and copies ran while one was open for 4% of the time, Pallas kernels for 0%

profile of v1, /device:TPU:0, one launch (start us, length us, event | category | flops | bytes accessed | tf_op | source)
XLA Modules:
  0.0 237.3 jit_solution(7463739314771961278)
XLA Ops:
  7.2 0.8 all_to_all.12
  8.0 15.5 %all_to_all.19 = s32[16,1,512]{2,1,0:T(1,128)S(1)} all-to-all(s32[16,1,512]{2,1,0:T(1,128)S(1)} %all_to_all.12), channel_id=1, replica_groups=mesh['table'=16,'narrow'=2] {'table'}, dimensions={0} | all-to-all | bytes 65536 | tf_op jit(solution)/shard_map/all_to_all | solution.py:36
  23.5 1.1 reshape.40
  24.6 2.0 slice_reduce_fusion.3
  26.6 6.1 %fusion.15 = bf16[2048,256]{1,0:T(8,128)(2,1)} fusion(bf16[1024,256]{1,0:T(8,128)(2,1)S(1)} %copy-done.2, s32[2048]{0:T(1024)S(1)} %get-tuple-element.21, s32[2048]{0:T(1024)S(1)} %get-tuple-element.22, s32[2048]{0:T(1024)S(1)} %get-tuple-element.23, s32[2048]{0:T(1024)S(1)} %get-tuple-element.20), kind=kOutput, calls=%fused_computation.18 | convolution fusion | flops 1107820544 | bytes 1605632 | tf_op jit(solution)/shard_map/dot_general | solution.py:42
  32.7 3.8 %all-to-all-start.1 = ((bf16[16,128,256]{2,1,0:T(8,128)(2,1)}), bf16[16,128,256]{2,1,0:T(8,128)(2,1)S(1)}, u32[]{:S(2)}, u32[]{:S(2)}) async-start(bf16[16,128,256]{2,1,0:T(8,128)(2,1)} %bitcast.1), calls=%async_computation.1 | async-start | bytes 2097152 | tf_op jit(solution)/shard_map/all_to_all | solution.py:44
  36.5 0.7 all-gather.5.cloned.1.call-update
  37.3 0.7 all-gather.7.cloned.1.call-update
  38.0 21.7 %all-to-all-done.1 = bf16[16,128,256]{2,1,0:T(8,128)(2,1)S(1)} async-done(((bf16[16,128,256]{2,1,0:T(8,128)(2,1)}), bf16[16,128,256]{2,1,0:T(8,128)(2,1)S(1)}, u32[]{:S(2)}, u32[]{:S(2)}) %all-to-all-start.1) | async-done | bytes 1048608 | tf_op jit(solution)/shard_map/all_to_all | solution.py:44
  59.8 1.5 fusion.23
  61.2 0.2 reshape.43
  61.5 1.5 convolution_convert_fusion.3
  63.1 2.0 fusion.29
  65.1 0.4 convolution_convert_fusion.2
  65.5 0.5 fusion.19
  66.0 0.2 reshape.44
  66.3 2.4 fusion.18
  68.6 31.3 %all_to_all.20 = bf16[16,128,256]{2,1,0:T(8,128)(2,1)S(1)} all-to-all(bf16[16,128,256]{2,1,0:T(8,128)(2,1)S(1)} %bitcast.23), channel_id=1, replica_groups=mesh['table'=16,'narrow'=2] {'table'}, dimensions={0} | all-to-all | bytes 2097152 | tf_op jit(solution)/shard_map/all_to_all | solution.py:93
  99.9 5.5 %fusion.20 = bf16[1024,256]{1,0:T(8,128)(2,1)} fusion(bf16[2048,256]{1,0:T(8,128)(2,1)S(1)} %bitcast.22, s32[2048]{0:T(1024)S(1)} %get-tuple-element.21, s32[2048]{0:T(1024)S(1)} %get-tuple-element.22, s32[2048]{0:T(1024)S(1)} %get-tuple-element.23, s32[2048]{0:T(1024)S(1)} %get-tuple-element.20), kind=kOutput, calls=%fused_computation.31 | convolution fusion | flops 1107558400 | bytes 1605632 | tf_op jit(solution)/shard_map/dot_general | solution.py:15
  105.5 0.5 convolution_convert_fusion.1
  106.0 0.5 convolution_convert_fusion
  106.5 1.6 pad_maximum_fusion
  108.2 4.8 %all-gather.9.cloned.1.call-done = bf16[2048,256]{1,0:T(8,128)(2,1)} async-done(((bf16[1024,256]{1,0:T(8,128)(2,1)}), bf16[2048,256]{1,0:T(8,128)(2,1)}) %all-gather.9.cloned.1.call-update) | async-done | bytes 1048592 | tf_op jit(solution)/shard_map/all_gather | solution.py:99
  112.9 1.7 reduce_sum.31
  114.9 0.7 dynamic_slice.3
  115.5 1.1 fusion.26
  116.6 9.2 %reduce-scatter.2.cloned.1.call-done = bf16[1024,512]{0,1:T(8,128)(2,1)} async-done(((bf16[2048,512]{0,1:T(8,128)(2,1)}), bf16[1024,512]{0,1:T(8,128)(2,1)}) %reduce-scatter.2.cloned.1.call-update) | async-done | bytes 1048592 | tf_op jit(solution)/shard_map/reduce_scatter | solution.py:73
  125.8 101.9 %all-reduce.1 = f32[1024,512]{0,1:T(8,128)S(1)} all-reduce(bf16[1024,512]{0,1:T(8,128)(2,1)} %reduce-scatter.2.cloned.1.call-done), channel_id=1, replica_groups=mesh['table'=16,'narrow'=2] {'table'}, use_global_device_ids=true, to_apply=%region_2.0 | all-reduce | flops 524288 | bytes 3145728 | tf_op jit(solution)/shard_map/psum | solution.py:81
  227.7 0.2 broadcast_multiply_fusion
  227.9 0.2 fusion.33
  228.2 1.3 copy.19
  229.5 1.3 copy.18
  (31 shorter events, 0.6 us)
Async XLA Ops:
  24.6 2.0 copy-start.2
  32.7 5.3 %copy-start.4 = (bf16[2048]{0:T(1024)(128)(2,1)S(1)}, bf16[2048]{0:T(1024)(128)(2,1)}, u32[]{:S(2)}) copy-start(bf16[2048]{0:T(1024)(128)(2,1)} %param.14) | copy-start | bytes 12292
  32.7 27.1 %copy-start.7 = (s32[16,128]{1,0:T(8,128)S(1)}, s32[16,128]{1,0:T(8,128)}, u32[]{:S(2)}) copy-start(s32[16,128]{1,0:T(8,128)} %param.17) | copy-start | bytes 24580
  32.7 27.1 %all-to-all-start.1 = ((bf16[16,128,256]{2,1,0:T(8,128)(2,1)}), bf16[16,128,256]{2,1,0:T(8,128)(2,1)S(1)}, u32[]{:S(2)}, u32[]{:S(2)}) async-start(bf16[16,128,256]{2,1,0:T(8,128)(2,1)} %bitcast.1), calls=%async_computation.1 | async-start | bytes 2097152 | tf_op jit(solution)/shard_map/all_to_all | solution.py:44
  36.5 25.0 %all-gather.5.cloned.1.call-start = ((), (), s32[]{:S(2)}) async-start(), calls=%async_computation.4 | async-start | bytes 1572864 | tf_op jit(solution)/shard_map/all_gather | solution.py:55
  37.2 25.9 %all-gather.7.cloned.1.call-start = ((), (), s32[]{:S(2)}) async-start(), calls=%async_computation.5 | async-start | bytes 1572864 | tf_op jit(solution)/shard_map/all_gather | solution.py:56
  38.0 75.0 %all-gather.9.cloned.1.call-start = ((), (), s32[]{:S(2)}) async-start(), calls=%async_computation.7 | async-start | bytes 1572864 | tf_op jit(solution)/shard_map/all_gather | solution.py:99
  61.2 1.9 copy-start.3
  61.5 3.6 %copy-start.8 = (f32[128]{0:T(128)S(1)}, f32[128]{0:T(128)}, u32[]{:S(2)}) copy-start(f32[128]{0:T(128)} %param.15) | copy-start | bytes 1540
  63.1 2.4 %copy-start = (bf16[2048,256]{1,0:T(8,128)(2,1)S(1)}, bf16[2048,256]{1,0:T(8,128)(2,1)}, u32[]{:S(2)}) copy-start(bf16[2048,256]{1,0:T(8,128)(2,1)} %all-gather.5.cloned.1.call-done) | copy-start | bytes 3145732
  63.1 2.0 copy-start.1
  65.1 0.9 copy-start.6
  105.5 20.4 %reduce-scatter.2.cloned.1.call-start = ((), (), s32[]{:S(2)}) async-start(), calls=%async_computation.6 | async-start | bytes 3145728 | tf_op jit(solution)/shard_map/reduce_scatter | solution.py:73
  108.1 6.7 %copy-start.5 = (f32[1024]{0:T(1024)S(1)}, f32[1024]{0:T(1024)}, u32[]{:S(2)}) copy-start(f32[1024]{0:T(1024)} %param.10) | copy-start | bytes 12292
Sparse Core Ops, SparseCore 0:
  38.9 10.2 all-gather.4
  50.7 10.1 all-gather.6
  105.6 7.2 all-gather.8
  115.0 10.7 reduce-scatter.1
